TPU v7x, 256 devices: a whole 4x4x8 slice. The times are simulated.
256 devices in a mesh: seq: 32 (over y, x, core), head: 8 (over z).
Axes of the slice: x: 4, y: 4, z: 8, core: 2. Of those that a mesh axis runs over, the one named last changes fastest.
Arguments:
- query_rows: bfloat16 [16384, 4096], P('seq', 'head'), may hold values from -6 to 6
- key_rows: bfloat16 [16384, 4096], P('seq', 'head'), may hold values from -6 to 6
- value_rows: bfloat16 [16384, 4096], P('seq', 'head'), may hold values from -6 to 6
- out_weight: bfloat16 [4096, 4096], P('seq', 'head'), may hold values from -0.09375 to 0.09375
- target_rows: bfloat16 [16384, 4096], P('seq', 'head'), may hold values from -6 to 6
Outputs:
- output: bfloat16 [16384, 4096], P('seq', 'head')
- grad_query: bfloat16 [16384, 4096], P('seq', 'head')
- grad_key: bfloat16 [16384, 4096], P('seq', 'head')
- grad_value: bfloat16 [16384, 4096], P('seq', 'head')
- grad_weight: float32 [4096, 4096], P('seq', 'head')
All inputs are finite; a program needn't handle non-finite values.
Results may differ from a plain program's by a relative error of at most 0.019.
Values may be sent and summed in bfloat16 or wider, within the bound.
A program may use at most 64 MiB of HBM per device.

v0:
```python
import math
import jax
import jax.numpy as jnp
from jax import lax
from jax.sharding import Mesh
from jax.sharding import PartitionSpec as P

DH = 128
BLK = 512
SEQ = ("seq_0", "seq_1", "seq_2")
EXACT = lax.Precision.HIGHEST


def filled_with(x, identity):
    return jnp.broadcast_to(jnp.asarray(identity, x.dtype), x.shape)


def entering(x, axes, combine, identity, reverse):
    before = start = filled_with(x, identity)
    so_far = x
    for axis in reversed(axes):
        devices, place = (lax.axis_size(axis), lax.axis_index(axis))
        pieces = lax.all_gather(so_far.astype(jnp.bfloat16), axis)
        inside, so_far = (start, start)
        for k in reversed(range(devices)) if reverse else range(devices):
            passed = k > place if reverse else k < place
            so_far = combine(so_far, pieces[k].astype(x.dtype))
            inside = jnp.where(passed, so_far, inside)
        before = combine(inside, before)
    return before


def add_states(earlier, later_one):
    return earlier + later_one


def on_device(query_rows, key_rows, value_rows, out_weight, target_rows):
    rows_dev = query_rows.shape[0]
    feature_width = query_rows.shape[1]
    local_heads = feature_width // DH
    block_count = rows_dev // BLK
    seq_count = lax.axis_size(SEQ)
    total_rows = rows_dev * seq_count
    seq_index = lax.axis_index(SEQ)
    positions = (seq_index * rows_dev + jnp.arange(rows_dev, dtype=jnp.int32) + 1).astype(
        jnp.float32
    )
    query_scale = lax.rsqrt(jnp.float32(DH) * positions)
    scaled = (query_rows.astype(jnp.float32) * query_scale[:, None]).astype(jnp.bfloat16)
    shaped = (block_count, BLK, local_heads, DH)
    query_blocks = scaled.reshape(shaped)
    key_blocks = key_rows.reshape(shaped)
    value_blocks = value_rows.reshape(shaped)
    causal = jnp.tril(jnp.ones((BLK, BLK), dtype=bool))
    empty_state = jnp.zeros((local_heads, DH, DH), jnp.float32)
    block_kv = jnp.einsum(
        "bshd,bshe->bhde", key_blocks, value_blocks, preferred_element_type=jnp.float32
    )
    local_total = jnp.sum(block_kv, axis=0)
    earlier = entering(local_total, SEQ, add_states, empty_state, False)
    running_kv = jnp.cumsum(block_kv, axis=0)
    before = earlier[None] + jnp.concatenate([jnp.zeros_like(block_kv), running_kv[:-1]], axis=0)
    inter = jnp.einsum("bthd,bhde->bthe", query_blocks.astype(jnp.float32), before, precision=EXACT)
    scores = jnp.einsum(
        "bthd,bshd->bhts", query_blocks, key_blocks, preferred_element_type=jnp.float32
    )
    scores = jnp.where(causal, scores, 0.0).astype(jnp.bfloat16)
    intra = jnp.einsum("bhts,bshe->bthe", scores, value_blocks, preferred_element_type=jnp.float32)
    attended = (inter + intra).astype(jnp.bfloat16).reshape(rows_dev, feature_width)
    whole_weight = lax.all_gather(out_weight, SEQ, axis=0, tiled=True)
    partial_out = lax.dot_general(
        attended, whole_weight, (((1,), (1,)), ((), ())), preferred_element_type=jnp.float32
    )
    summed = lax.psum_scatter(
        partial_out.astype(jnp.bfloat16), "head", scatter_dimension=1, tiled=True
    )
    residual = (summed.astype(jnp.float32) - target_rows.astype(jnp.float32)).astype(jnp.bfloat16)
    residual_full = lax.all_gather(residual, "head", axis=1, tiled=True)
    grad_attended = jnp.dot(residual_full, whole_weight, preferred_element_type=jnp.float32).astype(
        jnp.bfloat16
    )
    weight_factor = 1.0 / math.sqrt(total_rows)
    product = lax.dot_general(
        residual_full, attended, (((0,), (0,)), ((), ())), preferred_element_type=jnp.float32
    )
    grad_weight = lax.psum_scatter(
        (product * weight_factor).astype(jnp.bfloat16), SEQ, scatter_dimension=0, tiled=True
    ).astype(jnp.float32)
    grad_blocks = grad_attended.reshape(shaped)
    block_qg = jnp.einsum(
        "bthd,bthe->bhde", query_blocks, grad_blocks, preferred_element_type=jnp.float32
    )
    local_grad = jnp.sum(block_qg, axis=0)
    later = entering(local_grad, SEQ, add_states, empty_state, True)
    running_qg = jnp.cumsum(block_qg[::-1], axis=0)[::-1]
    after = later[None] + jnp.concatenate([running_qg[1:], jnp.zeros_like(block_qg)], axis=0)
    mixed = jnp.einsum(
        "bthe,bshe->bhts", grad_blocks, value_blocks, preferred_element_type=jnp.float32
    )
    mixed = jnp.where(causal, mixed, 0.0).astype(jnp.bfloat16)
    grad_scaled = jnp.einsum(
        "bthe,bhde->bthd", grad_blocks.astype(jnp.float32), before, precision=EXACT
    )
    grad_scaled = grad_scaled + jnp.einsum(
        "bhts,bshd->bthd", mixed, key_blocks, preferred_element_type=jnp.float32
    )
    grad_key = jnp.einsum(
        "bshe,bhde->bshd", value_blocks.astype(jnp.float32), after, precision=EXACT
    )
    grad_key = grad_key + jnp.einsum(
        "bhts,bthd->bshd", mixed, query_blocks, preferred_element_type=jnp.float32
    )
    grad_value = jnp.einsum(
        "bshd,bhde->bshe", key_blocks.astype(jnp.float32), after, precision=EXACT
    )
    grad_value = grad_value + jnp.einsum(
        "bhts,bthe->bshe", scores, grad_blocks, preferred_element_type=jnp.float32
    )
    grad_query = (grad_scaled.reshape(rows_dev, feature_width) * query_scale[:, None]).astype(
        jnp.bfloat16
    )
    return (
        summed,
        grad_query,
        grad_key.astype(jnp.bfloat16).reshape(rows_dev, feature_width),
        grad_value.astype(jnp.bfloat16).reshape(rows_dev, feature_width),
        grad_weight,
    )


def solution(mesh):
    torus = Mesh(
        mesh.devices.reshape(4, 4, 2, mesh.shape["head"]), ("seq_0", "seq_1", "seq_2", "head")
    )
    return jax.shard_map(
        on_device,
        mesh=torus,
        in_specs=(P(SEQ, "head"), P(SEQ, "head"), P(SEQ, "head"), P(SEQ, "head"), P(SEQ, "head")),
        out_specs=(P(SEQ, "head"), P(SEQ, "head"), P(SEQ, "head"), P(SEQ, "head"), P(SEQ, "head")),
        check_vma=False,
    )
```

profile of v0, /device:TPU:2, one launch (start us, length us, event | category | flops | bytes accessed | tf_op | source)
XLA Modules:
  0.0 285.8 jit_solution(8579663501388462409)
XLA Ops:
  7.2 0.0 copy-start
  7.2 0.0 all-gather.5.cloned.1.call-start
  7.2 0.7 all-gather.5.cloned.1.call-update
  7.9 0.0 reduce-scatter.3.cloned.1.call-start
  8.0 1.3 copy.82
  9.2 0.0 copy-start.5
  9.3 1.4 multiply_convert_fusion.2
  10.7 0.2 copy.55
  10.9 0.0 copy-done
  10.9 0.3 convolution_convert_fusion.3
  11.2 2.0 all-gather
  13.2 0.1 iota_compare_fusion
  13.3 0.0 copy-start.7
  13.3 12.8 %all_gather.31 = bf16[4,4,128,128]{3,2,1,0:T(8,128)(2,1)S(1)} all-gather(bf16[1,4,128,128]{3,2,1,0:T(8,128)(2,1)S(1)} %fusion.41), channel_id=1, replica_groups=mesh['seq_0'=4,'seq_1'=4,'seq_2'=2,'head'=8] {'seq_1'}, dimensions={0}, use_global_device_ids=true | all-gather | bytes 655360 | tf_op jit(solution)/shard_map/all_gather | solution.py:23
  26.2 0.1 fusion.40
  26.2 15.3 %all_gather.32 = bf16[4,4,128,128]{3,2,1,0:T(8,128)(2,1)S(1)} all-gather(bf16[1,4,128,128]{3,2,1,0:T(8,128)(2,1)S(1)} %fusion.40), channel_id=1, replica_groups=mesh['seq_0'=4,'seq_1'=4,'seq_2'=2,'head'=8] {'seq_0'}, dimensions={0}, use_global_device_ids=true | all-gather | bytes 655360 | tf_op jit(solution)/shard_map/all_gather | solution.py:23
  41.6 0.3 fusion.20
  41.8 0.0 copy-done.5
  41.8 0.0 copy-start.3
  41.8 2.0 select_convert_fusion.1
  43.8 0.8 convolution_bitcast_fusion.1
  44.6 0.0 copy-done.7
  44.7 0.0 copy-done.3
  44.7 1.4 fusion
  46.1 18.6 %all-gather.5.cloned.1.call-done = bf16[4096,512]{1,0:T(8,128)(2,1)} async-done(((bf16[128,512]{1,0:T(8,128)(2,1)}), bf16[4096,512]{1,0:T(8,128)(2,1)}) %all-gather.5.cloned.1.call-update) | async-done | bytes 4194320 | tf_op jit(solution)/shard_map/all_gather | solution.py:70
  64.7 6.7 %convolution_convert_fusion = bf16[512,4096]{1,0:T(8,128)(2,1)} fusion(bf16[512,512]{0,1:T(8,128)(2,1)} %bitcast.114, bf16[4096,512]{1,0:T(8,128)(2,1)} %all-gather.5.cloned.1.call-done), kind=kOutput, calls=%fused_computation.1 | convolution fusion | flops 2149580800 | bytes 8912896 | tf_op jit(solution)/shard_map/dot_general | solution.py:71
  71.5 0.0 reduce-scatter.3.cloned.1.call-update
  71.5 0.0 all-gather.7.cloned.1.call-start
  71.5 55.2 %reduce-scatter.3.cloned.1.call-done = bf16[512,512]{1,0:T(8,128)(2,1)} async-done(((bf16[512,4096]{1,0:T(8,128)(2,1)}), bf16[512,512]{1,0:T(8,128)(2,1)}) %reduce-scatter.3.cloned.1.call-update) | async-done | bytes 524304 | tf_op jit(solution)/shard_map/reduce_scatter | solution.py:74
  126.7 2.1 subtract_convert_fusion
  128.9 0.0 all-gather.7.cloned.1.call-update
  128.9 0.0 reduce-scatter.5.cloned.1.call-start
  128.9 53.6 %all-gather.7.cloned.1.call-done = bf16[512,4096]{1,0:T(8,128)(2,1)} async-done(((bf16[512,512]{1,0:T(8,128)(2,1)}), bf16[512,4096]{1,0:T(8,128)(2,1)}) %all-gather.7.cloned.1.call-update) | async-done | bytes 4194320 | tf_op jit(solution)/shard_map/all_gather | solution.py:78
  182.5 6.7 %multiply_convert_fusion = bf16[4096,512]{1,0:T(8,128)(2,1)} fusion(bf16[512,4096]{1,0:T(8,128)(2,1)} %all-gather.7.cloned.1.call-done, bf16[512,512]{0,1:T(8,128)(2,1)} %bitcast.115), kind=kOutput, calls=%fused_computation | convolution fusion | flops 2151677952 | bytes 8912896 | tf_op jit(solution)/shard_map/dot_general | solution.py:83
  189.2 0.0 reduce-scatter.5.cloned.1.call-update
  189.3 5.8 %convolution_convert_fusion.1 = bf16[512,512]{0,1:T(8,128)(2,1)S(1)} fusion(bf16[512,4096]{1,0:T(8,128)(2,1)} %all-gather.7.cloned.1.call-done, bf16[4096,512]{1,0:T(8,128)(2,1)} %all-gather.5.cloned.1.call-done), kind=kOutput, calls=%fused_computation.10 | convolution fusion | flops 2147745792 | bytes 8912896 | tf_op jit(solution)/shard_map/dot_general | solution.py:79
  195.1 0.0 copy-start.1
  195.1 0.3 convolution_convert_fusion.2
  195.4 0.0 copy-start.6
  195.4 2.1 all-gather.1
  197.6 13.5 %all_gather.36 = bf16[4,4,128,128]{3,2,1,0:T(8,128)(2,1)S(1)} all-gather(bf16[1,4,128,128]{3,2,1,0:T(8,128)(2,1)S(1)} %fusion.42), channel_id=1, replica_groups=mesh['seq_0'=4,'seq_1'=4,'seq_2'=2,'head'=8] {'seq_1'}, dimensions={0}, use_global_device_ids=true | all-gather | bytes 655360 | tf_op jit(solution)/shard_map/all_gather | solution.py:23
  211.1 0.1 fusion.39
  211.2 13.5 %all_gather.37 = bf16[4,4,128,128]{3,2,1,0:T(8,128)(2,1)S(1)} all-gather(bf16[1,4,128,128]{3,2,1,0:T(8,128)(2,1)S(1)} %fusion.39), channel_id=1, replica_groups=mesh['seq_0'=4,'seq_1'=4,'seq_2'=2,'head'=8] {'seq_0'}, dimensions={0}, use_global_device_ids=true | all-gather | bytes 655360 | tf_op jit(solution)/shard_map/all_gather | solution.py:23
  224.7 0.3 fusion.29
  224.9 0.4 fusion.44
  225.4 0.0 copy-done.1
  225.4 0.0 copy-done.6
  225.4 0.6 fusion.2
  226.0 1.0 copy.49
  227.0 1.9 select_convert_fusion
  229.0 0.4 fusion.43
  229.4 0.0 copy-start.2
  229.4 1.4 fusion.1
  230.8 0.0 copy-start.4
  230.8 2.1 copy.48
  232.9 1.8 convolution_bitcast_fusion
  234.8 0.0 copy-done.2
  234.8 0.0 copy-done.4
  234.8 0.6 convolution_add_fusion.2
  235.4 0.3 copy.41
  235.7 0.9 multiply_convert_fusion.1
  236.7 41.0 %reduce-scatter.5.cloned.1.call-done = bf16[128,512]{1,0:T(8,128)(2,1)} async-done(((bf16[4096,512]{1,0:T(8,128)(2,1)}), bf16[128,512]{1,0:T(8,128)(2,1)}) %reduce-scatter.5.cloned.1.call-update) | async-done | bytes 131088 | tf_op jit(solution)/shard_map/reduce_scatter | solution.py:86
  277.6 1.6 convert_element_type.247
  (3 shorter events, 0.1 us)
Async XLA Ops:
  7.2 3.7 %copy-start = (bf16[512,512]{1,0:T(8,128)(2,1)S(1)}, bf16[512,512]{1,0:T(8,128)(2,1)}, u32[]{:S(2)}) copy-start(bf16[512,512]{1,0:T(8,128)(2,1)} %param.7) | copy-start | bytes 1572868
  7.2 57.6 %all-gather.5.cloned.1.call-start = ((), (), s32[]{:S(2)}) async-start(), calls=%async_computation.2 | async-start | bytes 4325376 | tf_op jit(solution)/shard_map/all_gather | solution.py:70
  7.9 118.8 %reduce-scatter.3.cloned.1.call-start = ((), (), s32[]{:S(2)}) async-start(), calls=%async_computation.3 | async-start | bytes 4718592 | tf_op jit(solution)/shard_map/reduce_scatter | solution.py:74
  9.2 32.6 %copy-start.5 = (bf16[512,512]{0,1:T(8,128)(2,1)}, bf16[512,512]{0,1:T(8,128)(2,1)S(1)}, u32[]{:S(2)}) copy-start(bf16[512,512]{0,1:T(8,128)(2,1)S(1)} %copy.82) | copy-start | bytes 1572868
  13.3 31.4 %copy-start.7 = (pred[512,512]{1,0:T(8,128)(4,1)}, pred[512,512]{1,0:T(8,128)(4,1)S(1)}, u32[]{:S(2)}) copy-start(pred[512,512]{1,0:T(8,128)(4,1)S(1)} %iota_compare_fusion) | copy-start | bytes 786436
  41.8 2.8 copy-start.3
  71.5 111.0 %all-gather.7.cloned.1.call-start = ((), (), s32[]{:S(2)}) async-start(), calls=%async_computation.4 | async-start | bytes 4718592 | tf_op jit(solution)/shard_map/all_gather | solution.py:78
  128.9 148.8 %reduce-scatter.5.cloned.1.call-start = ((), (), s32[]{:S(2)}) async-start(), calls=%async_computation.5 | async-start | bytes 4325376 | tf_op jit(solution)/shard_map/reduce_scatter | solution.py:86
  195.1 30.3 %copy-start.1 = (bf16[512,512]{0,1:T(8,128)(2,1)}, bf16[512,512]{0,1:T(8,128)(2,1)S(1)}, u32[]{:S(2)}) copy-start(bf16[512,512]{0,1:T(8,128)(2,1)S(1)} %convolution_convert_fusion.1) | copy-start | bytes 1572868
  195.4 30.0 %copy-start.6 = (bf16[512,512]{1,0:T(8,128)(2,1)S(1)}, bf16[512,512]{1,0:T(8,128)(2,1)}, u32[]{:S(2)}) copy-start(bf16[512,512]{1,0:T(8,128)(2,1)} %param.6) | copy-start | bytes 1572868
  229.4 5.3 %copy-start.2 = (bf16[512,512]{0,1:T(8,128)(2,1)S(1)}, bf16[512,512]{0,1:T(8,128)(2,1)}, u32[]{:S(2)}) copy-start(bf16[512,512]{0,1:T(8,128)(2,1)} %copy-done.1) | copy-start | bytes 1572868
  230.8 4.0 %copy-start.4 = (f32[4,128,128]{2,1,0:T(8,128)S(1)}, f32[4,128,128]{2,1,0:T(8,128)}, u32[]{:S(2)}) copy-start(f32[4,128,128]{2,1,0:T(8,128)} %copy-done.3) | copy-start | bytes 786436
Sparse Core Ops, SparseCore 0:
  10.5 54.1 all-gather.4
  71.6 55.0 reduce-scatter.2
  129.1 53.3 all-gather.6
  189.3 88.2 reduce-scatter.4
where the time goes:
time: 286 us
  waiting for transfers between devices  169 us (59%)
  blocking collectives  59.3 us (21%)
  matrix products  31.3 us (11%)
  between operations  14.1 us (5%)
  other arithmetic  6.88 us (2%)
  local copies, waits for them, and re-layouts  4.94 us (2%)
    all_gather x6, blocking collectives, entering(): pieces = lax.all_gather(so_far.astype(jnp.bfloat16), axis)  59.3 us
    reduce_scatter x1, waiting for transfers between devices, on_device(): lax.psum_scatter(partial_out.astype(jnp.bfloat16), 'head', scatter_dimens...  55.2 us
    all_gather x1, waiting for transfers between devices, on_device(): residual_full = lax.all_gather(residual, 'head', axis=1, tiled=True)  53.6 us
    reduce_scatter x1, waiting for transfers between devices, on_device(): lax.psum_scatter((product * weight_factor).astype(jnp.bfloat16), SEQ, sca...  41 us
    all_gather x1, waiting for transfers between devices, on_device(): whole_weight = lax.all_gather(out_weight, SEQ, axis=0, tiled=True)  18.6 us
    dot_general x1, matrix products, on_device(): lax.dot_general(attended, whole_weight, (((1,), (1,)), ((), ())), preferr...  6.73 us
    dot_general x1, matrix products, on_device(): lax.dot_general(residual_full, attended, (((0,), (0,)), ((), ())), prefer...  6.68 us
    dot_general x1, matrix products, on_device(): jnp.dot(residual_full, whole_weight, preferred_element_type=jnp.float32)  5.84 us
  transfers between devices with their start and end apart: 4, of which 4 were waited for; matrix products, arithmetic and copies ran while one was open for 9% of the time, Pallas kernels for 0%

commit v1 on v0

--- a/solution.py
+++ b/solution.py
@@ -75,7 +75,9 @@
         partial_out.astype(jnp.bfloat16), "head", scatter_dimension=1, tiled=True
     )
     residual = (summed.astype(jnp.float32) - target_rows.astype(jnp.float32)).astype(jnp.bfloat16)
-    residual_full = lax.all_gather(residual, "head", axis=1, tiled=True)
+    residual_full = jnp.concatenate(
+        lax.all_to_all(jnp.stack([residual] * lax.axis_size("head")), "head", 0, 0), axis=1
+    )
     grad_attended = jnp.dot(residual_full, whole_weight, preferred_element_type=jnp.float32).astype(
         jnp.bfloat16
     )

time: 286 us -> 334 us (1.17)
  blocking collectives: 59.3 us -> 160 us
  waiting for transfers between devices: 169 us -> 113 us
  local copies, waits for them, and re-layouts: 4.94 us -> 10.4 us
    all_to_all x0 -> x1, blocking collectives: none -> 100 us  [on_device(): lax.all_to_all(jnp.stack([residual] * lax.axis_size('head')), 'head', 0, 0)]
    all_gather x1 -> x0, waiting for transfers between devices: 53.6 us -> none  [on_device(): residual_full = lax.all_gather(residual, 'head', axis=1, tiled=True)]
  transfers between devices with their start and end apart: 4 -> 3, of which waited for: 4 -> 3; matrix products, arithmetic and copies ran while one was open for 9% -> 8% of each run, Pallas kernels for 0% -> 0%
where the time goes in v1:
time: 334 us; the launch traced here: 333 us
  blocking collectives  160 us (48%)
  waiting for transfers between devices  113 us (34%)
  matrix products  29.1 us (9%)
  between operations  14.1 us (4%)
  local copies, waits for them, and re-layouts  10.4 us (3%)
  other arithmetic  6.88 us (2%)
    all_to_all x1, blocking collectives, on_device(): lax.all_to_all(jnp.stack([residual] * lax.axis_size('head')), 'head', 0, 0)  100 us
    all_gather x6, blocking collectives, entering(): pieces = lax.all_gather(so_far.astype(jnp.bfloat16), axis)  59.3 us
    reduce_scatter x1, waiting for transfers between devices, on_device(): lax.psum_scatter(partial_out.astype(jnp.bfloat16), 'head', scatter_dimens...  55.2 us
    reduce_scatter x1, waiting for transfers between devices, on_device(): lax.psum_scatter((product * weight_factor).astype(jnp.bfloat16), SEQ, sca...  38.5 us
    all_gather x1, waiting for transfers between devices, on_device(): whole_weight = lax.all_gather(out_weight, SEQ, axis=0, tiled=True)  18.6 us
    dot_general x1, matrix products, on_device(): lax.dot_general(attended, whole_weight, (((1,), (1,)), ((), ())), preferr...  6.74 us
  transfers between devices with their start and end apart: 3, of which 3 were waited for; matrix products, arithmetic and copies ran while one was open for 8% of the time, Pallas kernels for 0%

profile of v1, /device:TPU:2, one launch (start us, length us, event | category | flops | bytes accessed | tf_op | source)
XLA Modules:
  0.0 333.2 jit_solution(11192329112444400963)
XLA Ops:
  7.2 0.0 copy-start
  7.2 0.0 all-gather.4.cloned.1.call-start
  7.2 0.7 all-gather.4.cloned.1.call-update
  7.9 0.0 reduce-scatter.3.cloned.1.call-start
  8.0 1.3 copy.104
  9.2 0.0 copy-start.6
  9.3 1.4 multiply_convert_fusion.2
  10.7 0.2 copy.77
  10.9 0.0 copy-done
  10.9 0.3 convolution_convert_fusion.3
  11.2 2.0 all-gather
  13.2 0.1 iota_compare_fusion
  13.3 0.0 copy-start.9
  13.3 12.8 %all_gather.28 = bf16[4,4,128,128]{3,2,1,0:T(8,128)(2,1)S(1)} all-gather(bf16[1,4,128,128]{3,2,1,0:T(8,128)(2,1)S(1)} %fusion.41), channel_id=1, replica_groups=mesh['seq_0'=4,'seq_1'=4,'seq_2'=2,'head'=8] {'seq_1'}, dimensions={0}, use_global_device_ids=true | all-gather | bytes 655360 | tf_op jit(solution)/shard_map/all_gather | solution.py:23
  26.2 0.1 fusion.40
  26.2 15.3 %all_gather.29 = bf16[4,4,128,128]{3,2,1,0:T(8,128)(2,1)S(1)} all-gather(bf16[1,4,128,128]{3,2,1,0:T(8,128)(2,1)S(1)} %fusion.40), channel_id=1, replica_groups=mesh['seq_0'=4,'seq_1'=4,'seq_2'=2,'head'=8] {'seq_0'}, dimensions={0}, use_global_device_ids=true | all-gather | bytes 655360 | tf_op jit(solution)/shard_map/all_gather | solution.py:23
  41.6 0.3 fusion.20
  41.8 0.0 copy-done.6
  41.8 0.0 copy-start.4
  41.8 2.0 select_convert_fusion.1
  43.8 0.8 convolution_bitcast_fusion.1
  44.6 0.0 copy-done.9
  44.7 0.0 copy-done.4
  44.7 1.4 fusion
  46.1 18.6 %all-gather.4.cloned.1.call-done = bf16[4096,512]{1,0:T(8,128)(2,1)} async-done(((bf16[128,512]{1,0:T(8,128)(2,1)}), bf16[4096,512]{1,0:T(8,128)(2,1)}) %all-gather.4.cloned.1.call-update) | async-done | bytes 4194320 | tf_op jit(solution)/shard_map/all_gather | solution.py:70
  64.7 6.7 %convolution_convert_fusion = bf16[512,4096]{1,0:T(8,128)(2,1)} fusion(bf16[512,512]{0,1:T(8,128)(2,1)} %bitcast.119, bf16[4096,512]{1,0:T(8,128)(2,1)} %all-gather.4.cloned.1.call-done), kind=kOutput, calls=%fused_computation.1 | convolution fusion | flops 2149580800 | bytes 8912896 | tf_op jit(solution)/shard_map/dot_general | solution.py:71
  71.5 0.0 reduce-scatter.3.cloned.1.call-update
  71.5 0.0 reduce-scatter.5.cloned.1.call-start
  71.5 55.2 %reduce-scatter.3.cloned.1.call-done = bf16[512,512]{1,0:T(8,128)(2,1)} async-done(((bf16[512,4096]{1,0:T(8,128)(2,1)}), bf16[512,512]{1,0:T(8,128)(2,1)}) %reduce-scatter.3.cloned.1.call-update) | async-done | bytes 524304 | tf_op jit(solution)/shard_map/reduce_scatter | solution.py:74
  126.7 2.1 subtract_convert_fusion
  128.9 2.0 copy.58
  130.9 1.4 stack.2
  132.3 0.0 copy-start.8
  132.3 100.3 %all_to_all.5 = bf16[8,512,512]{1,2,0:T(8,128)(2,1)S(1)} all-to-all(bf16[8,512,512]{1,2,0:T(8,128)(2,1)S(1)} %stack.2), channel_id=1, replica_groups=mesh['seq_0'=4,'seq_1'=4,'seq_2'=2,'head'=8] {'head'}, dimensions={0} | all-to-all | bytes 8388608 | tf_op jit(solution)/shard_map/all_to_all | solution.py:79
  232.7 2.0 copy-done.3
  234.6 0.0 copy-done.8
  234.6 4.4 %multiply_convert_fusion = bf16[4096,512]{1,0:T(8,128)(2,1)} fusion(bf16[512,4096]{0,1:T(8,128)(2,1)S(1)} %bitcast.112, bf16[512,512]{0,1:T(8,128)(2,1)S(1)} %bitcast.120), kind=kOutput, calls=%fused_computation | convolution fusion | flops 2151677952 | bytes 8912896 | tf_op jit(solution)/shard_map/dot_general | solution.py:85
  239.1 0.0 reduce-scatter.5.cloned.1.call-update
  239.1 5.8 %convolution_convert_fusion.1 = bf16[512,512]{0,1:T(8,128)(2,1)S(1)} fusion(bf16[512,4096]{0,1:T(8,128)(2,1)} %bitcast.113, bf16[4096,512]{1,0:T(8,128)(2,1)} %all-gather.4.cloned.1.call-done), kind=kOutput, calls=%fused_computation.10 | convolution fusion | flops 2147745792 | bytes 8912896 | tf_op jit(solution)/shard_map/dot_general | solution.py:81
  245.0 0.0 copy-start.1
  245.0 0.3 convolution_convert_fusion.2
  245.3 0.0 copy-start.7
  245.3 2.3 all-gather.1
  247.7 13.5 %all_gather.32 = bf16[4,4,128,128]{3,2,1,0:T(8,128)(2,1)S(1)} all-gather(bf16[1,4,128,128]{3,2,1,0:T(8,128)(2,1)S(1)} %fusion.42), channel_id=1, replica_groups=mesh['seq_0'=4,'seq_1'=4,'seq_2'=2,'head'=8] {'seq_1'}, dimensions={0}, use_global_device_ids=true | all-gather | bytes 655360 | tf_op jit(solution)/shard_map/all_gather | solution.py:23
  261.2 0.1 fusion.39
  261.3 13.3 %all_gather.33 = bf16[4,4,128,128]{3,2,1,0:T(8,128)(2,1)S(1)} all-gather(bf16[1,4,128,128]{3,2,1,0:T(8,128)(2,1)S(1)} %fusion.39), channel_id=1, replica_groups=mesh['seq_0'=4,'seq_1'=4,'seq_2'=2,'head'=8] {'seq_0'}, dimensions={0}, use_global_device_ids=true | all-gather | bytes 655360 | tf_op jit(solution)/shard_map/all_gather | solution.py:23
  274.6 0.3 fusion.29
  274.8 0.4 fusion.44
  275.3 0.0 copy-done.1
  275.3 0.6 fusion.2
  275.9 1.0 copy.71
  276.9 1.9 select_convert_fusion
  278.9 0.4 fusion.43
  279.3 0.0 copy-start.2
  279.3 1.4 fusion.1
  280.7 2.1 copy.70
  282.8 1.8 convolution_bitcast_fusion
  284.7 0.0 copy-done.2
  284.7 0.0 copy-done.5
  284.7 0.6 convolution_add_fusion.2
  285.3 0.3 copy.63
  285.6 0.9 multiply_convert_fusion.1
  286.5 38.5 %reduce-scatter.5.cloned.1.call-done = bf16[128,512]{1,0:T(8,128)(2,1)} async-done(((bf16[4096,512]{1,0:T(8,128)(2,1)}), bf16[128,512]{1,0:T(8,128)(2,1)}) %reduce-scatter.5.cloned.1.call-update) | async-done | bytes 131088 | tf_op jit(solution)/shard_map/reduce_scatter | solution.py:88
  325.1 1.6 convert_element_type.247
  (6 shorter events, 0.1 us)
Async XLA Ops:
  7.2 3.7 %copy-start = (bf16[512,512]{1,0:T(8,128)(2,1)S(1)}, bf16[512,512]{1,0:T(8,128)(2,1)}, u32[]{:S(2)}) copy-start(bf16[512,512]{1,0:T(8,128)(2,1)} %param.7) | copy-start | bytes 1572868
  7.2 57.6 %all-gather.4.cloned.1.call-start = ((), (), s32[]{:S(2)}) async-start(), calls=%async_computation.3 | async-start | bytes 4325376 | tf_op jit(solution)/shard_map/all_gather | solution.py:70
  7.9 118.8 %reduce-scatter.3.cloned.1.call-start = ((), (), s32[]{:S(2)}) async-start(), calls=%async_computation.4 | async-start | bytes 4718592 | tf_op jit(solution)/shard_map/reduce_scatter | solution.py:74
  9.2 32.6 %copy-start.6 = (bf16[512,512]{0,1:T(8,128)(2,1)}, bf16[512,512]{0,1:T(8,128)(2,1)S(1)}, u32[]{:S(2)}) copy-start(bf16[512,512]{0,1:T(8,128)(2,1)S(1)} %copy.104) | copy-start | bytes 1572868
  13.3 31.4 %copy-start.9 = (pred[512,512]{1,0:T(8,128)(4,1)}, pred[512,512]{1,0:T(8,128)(4,1)S(1)}, u32[]{:S(2)}) copy-start(pred[512,512]{1,0:T(8,128)(4,1)S(1)} %iota_compare_fusion) | copy-start | bytes 786436
  41.8 2.8 copy-start.4
  71.5 253.6 %reduce-scatter.5.cloned.1.call-start = ((), (), s32[]{:S(2)}) async-start(), calls=%async_computation.5 | async-start | bytes 4325376 | tf_op jit(solution)/shard_map/reduce_scatter | solution.py:88
  132.3 102.3 %copy-start.8 = (bf16[4,128,512]{2,1,0:T(8,128)(2,1)S(1)}, bf16[4,128,512]{2,1,0:T(8,128)(2,1)}, u32[]{:S(2)}) copy-start(bf16[4,128,512]{2,1,0:T(8,128)(2,1)} %fusion) | copy-start | bytes 1572868
  232.7 2.0 copy-start.3
  245.0 30.3 %copy-start.1 = (bf16[512,512]{0,1:T(8,128)(2,1)}, bf16[512,512]{0,1:T(8,128)(2,1)S(1)}, u32[]{:S(2)}) copy-start(bf16[512,512]{0,1:T(8,128)(2,1)S(1)} %convolution_convert_fusion.1) | copy-start | bytes 1572868
  245.3 30.0 %copy-start.7 = (bf16[512,512]{1,0:T(8,128)(2,1)S(1)}, bf16[512,512]{1,0:T(8,128)(2,1)}, u32[]{:S(2)}) copy-start(bf16[512,512]{1,0:T(8,128)(2,1)} %param.6) | copy-start | bytes 1572868
  279.3 5.3 %copy-start.2 = (bf16[512,512]{0,1:T(8,128)(2,1)S(1)}, bf16[512,512]{0,1:T(8,128)(2,1)}, u32[]{:S(2)}) copy-start(bf16[512,512]{0,1:T(8,128)(2,1)} %copy-done.1) | copy-start | bytes 1572868
  280.7 4.0 %copy-start.5 = (f32[4,128,128]{2,1,0:T(8,128)S(1)}, f32[4,128,128]{2,1,0:T(8,128)}, u32[]{:S(2)}) copy-start(f32[4,128,128]{2,1,0:T(8,128)} %copy-done.4) | copy-start | bytes 786436
Sparse Core Ops, SparseCore 0:
  10.5 54.1 all-gather.3
  71.6 55.0 reduce-scatter.2
  239.2 85.7 reduce-scatter.4
